TPU v7x, 32 devices: a whole 2x2x4 slice. The times are simulated.
32 devices in a mesh: groups: 2 (over y), wide: 4 (over x, core), tp: 4 (over z).
Axes of the slice: x: 2, y: 2, z: 4, core: 2. Of those that a mesh axis runs over, the one named last changes fastest.
Arguments:
- patches: bfloat16 [2048, 1280], P(('groups', 'wide')), parts along dimension 0, may hold values from -190 to 190
- patch_counts: int32 [64], P('groups'), parts along dimension 0, may hold values from 24 to 32, as said below
- placement: int32 [64, 2], P('groups'), parts along dimension 0, may hold values from 0 to 511, as said below
- positions: int32 [3, 4096], P(None, ('groups', 'wide')), parts along dimension 1, may hold values from 0 to 2047
- text_embeds: bfloat16 [4096, 8192], P(('groups', 'wide'), 'tp'), parts along dimension 0, may hold values from -180 to 180
- vit_gain: float32 [1280], replicated, may hold values from 0.1 to 1.9
- vit_qkv: bfloat16 [1280, 3, 1280], P(None, None, 'tp'), may hold values from -4 to 4
- vit_proj: bfloat16 [1280, 1280], P('tp'), may hold values from -0.15625 to 0.15625
- merger_gain: float32 [1280], replicated, may hold values from 0.1 to 1.9
- merger_up: bfloat16 [5120, 2560], P(None, 'tp'), may hold values from -0.078125 to 0.078125
- merger_down: bfloat16 [2560, 8192], P('tp'), may hold values from -0.15625 to 0.15625
- llm_gain: float32 [8192], replicated, may hold values from 0.1 to 1.9
- llm_query: bfloat16 [8192, 4096], P('wide', 'tp'), may hold values from -0.0625 to 0.0625
- llm_key: bfloat16 [8192, 1024], P('wide', 'tp'), may hold values from -0.0625 to 0.0625
- llm_value: bfloat16 [8192, 1024], P('wide', 'tp'), may hold values from -0.0625 to 0.0625
Outputs:
- query: bfloat16 [4096, 4096], P(('groups', 'wide'), 'tp'), parts along dimension 0
- key_cache: bfloat16 [4096, 1024], P(('groups', 'wide'), 'tp'), parts along dimension 0
- value_cache: bfloat16 [4096, 1024], P(('groups', 'wide'), 'tp'), parts along dimension 0
There are 2 independent parts, one for each index of `groups`. A program takes and returns all parts, laid end to end along the dimension named above; an argument that names none is the same for every part. Nothing has to cross between parts.
Inputs may be any that keep to these rules, and one draw needn't show every extreme that they name: `patch_counts`: each count is a multiple of 4; images 8 * s to 8 * s + 7 belong to encoder device s of the wide axis; patch rows 4 m to 4 m + 3 of an image form its merged row m. `placement`: column 0 is the owner on the wide axis, column 1 the first of the image's merged rows among that owner's 512 rows. Images' merged rows never intersect and stay within the owner's rows. Each owner receives 8 images. At most 16 merged rows go from one encoder device to one owner, and that number is reached in every draw.
All inputs are finite; a program needn't handle non-finite values.
Results may differ from a plain program's by a relative error of at most 0.015.
Values may be sent and summed in bfloat16 or wider, within the bound.
No kernel may reach another device: no remote copies, remote signals or barrier semaphores. Data moves between devices by JAX's collectives and lax.ppermute only.
A program may use at most 128 MiB of HBM per device.

v0:
```python
import jax
import jax.numpy as jnp
from jax import lax
from jax.sharding import PartitionSpec as P

VD = 1280
HD = 128
IMG_DEV = 8
MAXP = 32
TOK_DEV = 512
VHD = 80
MAXM = 8
NORM_EPS = 1e-06
ROPE_BASE = 1000000.0


def layer_norm(inputs, scale_gain):
    center = jnp.mean(inputs, axis=-1, keepdims=True)
    shifted = inputs - center
    spread = jnp.mean(shifted * shifted, axis=-1, keepdims=True)
    return shifted * lax.rsqrt(spread + NORM_EPS) * scale_gain


def rms_norm(inputs, scale_gain):
    square = jnp.mean(inputs * inputs, axis=-1, keepdims=True)
    return inputs * lax.rsqrt(square + NORM_EPS) * scale_gain


def rotary(values, positions):
    half_size = HD // 2
    frequency = jnp.arange(half_size).astype(jnp.float32)
    inverse = ROPE_BASE ** (-2.0 * frequency / HD)
    first_end = HD // 8
    second = first_end + 3 * HD // 16
    ordinal = jnp.arange(half_size)
    section = jnp.where(ordinal < first_end, 0, jnp.where(ordinal < second, 1, 2))
    chosen = jnp.where(
        section[:, None] == 0,
        positions[0][None, :],
        jnp.where(section[:, None] == 1, positions[1][None, :], positions[2][None, :]),
    )
    angles = chosen.T.astype(jnp.float32) * inverse[None, :]
    angles = jnp.concatenate([angles, angles], axis=1)
    cosine = jnp.cos(angles)[:, None, :]
    sine_table = jnp.sin(angles)[:, None, :]
    upper_half = values[..., :half_size]
    lower_half = values[..., half_size:]
    turned = jnp.concatenate([-lower_half, upper_half], axis=-1)
    return values * cosine + turned * sine_table


def handoff_tables(patch_counts, placement, width_wide, myself, capacity):
    merged_count = patch_counts // 4
    owners = placement[:, 0]
    starts = placement[:, 1]
    owner_grid = owners.reshape(width_wide, IMG_DEV)
    count_grid = merged_count.reshape(width_wide, IMG_DEV)
    ordinal = jnp.arange(IMG_DEV)
    before = ordinal[:, None] < ordinal[None, :]
    same_owner = owner_grid[:, :, None] == owner_grid[:, None, :]
    offsets = jnp.sum(jnp.where(same_owner & before[None], count_grid[:, :, None], 0), axis=1)
    mine_owner = lax.dynamic_index_in_dim(owner_grid, myself, 0, keepdims=False)
    mine_count = lax.dynamic_index_in_dim(count_grid, myself, 0, keepdims=False)
    mine_offset = lax.dynamic_index_in_dim(offsets, myself, 0, keepdims=False)
    target = jnp.arange(width_wide)[:, None, None]
    slot_index = jnp.arange(capacity)[None, :, None]
    matches = (
        (mine_owner[None, None, :] == target)
        & (slot_index >= mine_offset[None, None, :])
        & (slot_index < mine_offset[None, None, :] + mine_count[None, None, :])
    )
    source_row = ordinal[None, None, :] * MAXM + slot_index - mine_offset[None, None, :]
    send_index = jnp.sum(jnp.where(matches, source_row, 0), axis=-1)
    send_live = jnp.any(matches, axis=-1)
    row_place = jnp.arange(TOK_DEV)[:, None]
    inside = (
        (owners[None, :] == myself)
        & (row_place >= starts[None, :])
        & (row_place < starts[None, :] + merged_count[None, :])
    )
    image_source = jnp.arange(owners.shape[0]) // IMG_DEV
    flat_slot = (
        image_source[None, :] * capacity
        + offsets.reshape(-1)[None, :]
        + row_place
        - starts[None, :]
    )
    take_index = jnp.sum(jnp.where(inside, flat_slot, 0), axis=-1)
    take_live = jnp.any(inside, axis=-1)
    return (send_index, send_live, take_index, take_live)


def pack_rows(visual, send_index, send_live):
    picked = jnp.take(visual, send_index.reshape(-1), axis=0)
    picked = picked.reshape(send_index.shape + (visual.shape[1],))
    return jnp.where(send_live[..., None], picked, jnp.zeros((), visual.dtype))


def place_rows(incoming, take_index, take_live, text_rows):
    flattened = incoming.reshape(-1, incoming.shape[-1])
    picked = jnp.take(flattened, take_index, axis=0)
    return jnp.where(take_live[:, None], picked, text_rows)


def per_device(
    patches,
    patch_counts,
    placement,
    positions,
    text_embeds,
    vit_gain,
    vit_qkv,
    vit_proj,
    merger_gain,
    merger_up,
    merger_down,
    llm_gain,
    llm_query,
    llm_key,
    llm_value,
):
    width_wide = lax.axis_size("wide")
    myself = lax.axis_index("wide")
    capacity = MAXM * ((IMG_DEV + width_wide - 1) // width_wide)
    local_heads = vit_qkv.shape[2] // VHD
    patch_rows = patches.astype(jnp.float32)
    normed = layer_norm(patch_rows, vit_gain).astype(jnp.bfloat16)
    triple = jnp.dot(normed, vit_qkv.reshape(VD, -1), preferred_element_type=jnp.float32).astype(
        jnp.bfloat16
    )
    triple = triple.reshape(IMG_DEV, MAXP, 3, local_heads, VHD)
    scores = jnp.einsum(
        "iqhd,ikhd->ihqk", triple[:, :, 0], triple[:, :, 1], preferred_element_type=jnp.float32
    ) * VHD ** (-0.5)
    own_counts = lax.dynamic_slice_in_dim(patch_counts, myself * IMG_DEV, IMG_DEV)
    present = jnp.arange(MAXP)[None, :] < own_counts[:, None]
    scores = jnp.where(present[:, None, None, :], scores, -jnp.inf)
    highest = jnp.max(scores, axis=-1, keepdims=True)
    raised = jnp.exp(scores - highest)
    attention_weights = (raised / jnp.sum(raised, axis=-1, keepdims=True)).astype(jnp.bfloat16)
    context = jnp.einsum(
        "ihqk,ikhd->iqhd", attention_weights, triple[:, :, 2], preferred_element_type=jnp.float32
    ).astype(jnp.bfloat16)
    context = context.reshape(IMG_DEV * MAXP, local_heads * VHD)
    partial_heads = jnp.dot(context, vit_proj, preferred_element_type=jnp.float32)
    attended = lax.psum(partial_heads.astype(jnp.bfloat16), "tp").astype(jnp.float32)
    mixed_rows = patch_rows + attended
    merged_in = (
        layer_norm(mixed_rows, merger_gain).astype(jnp.bfloat16).reshape(IMG_DEV * MAXM, 4 * VD)
    )
    hidden = jax.nn.gelu(
        jnp.dot(merged_in, merger_up, preferred_element_type=jnp.float32), approximate=False
    ).astype(jnp.bfloat16)
    partial_visual = jnp.dot(hidden, merger_down, preferred_element_type=jnp.float32)
    send_index, send_live, take_index, take_live = handoff_tables(
        patch_counts, placement, width_wide, myself, capacity
    )
    visual = lax.psum_scatter(
        partial_visual.astype(jnp.bfloat16), "tp", scatter_dimension=1, tiled=True
    )
    outgoing = pack_rows(visual, send_index, send_live)
    incoming = lax.all_to_all(outgoing, "wide", split_axis=0, concat_axis=0, tiled=True)
    prompt_slice = place_rows(incoming, take_index, take_live, text_embeds)
    prompt_rows = lax.all_gather(prompt_slice, "tp", axis=1, tiled=True)
    normed_prompt = rms_norm(prompt_rows.astype(jnp.float32), llm_gain).astype(jnp.bfloat16)
    weight_rows = (
        lax.all_gather(llm_query, "wide", axis=0, tiled=True),
        lax.all_gather(llm_key, "wide", axis=0, tiled=True),
        lax.all_gather(llm_value, "wide", axis=0, tiled=True),
    )
    projected_query, projected_key, projected_value = tuple(
        (
            jnp.dot(normed_prompt, matrix_rows, preferred_element_type=jnp.float32)
            for matrix_rows in weight_rows
        )
    )
    queries = (
        rotary(projected_query.reshape(TOK_DEV, -1, HD), positions)
        .astype(jnp.bfloat16)
        .reshape(TOK_DEV, -1)
    )
    key_rows = (
        rotary(projected_key.reshape(TOK_DEV, -1, HD), positions)
        .astype(jnp.bfloat16)
        .reshape(TOK_DEV, -1)
    )
    value_rows = projected_value.astype(jnp.bfloat16)
    return (queries, key_rows, value_rows)


def solution(mesh):
    return jax.shard_map(
        per_device,
        mesh=mesh,
        in_specs=(
            P(("groups", "wide"), None),
            P("groups"),
            P("groups", None),
            P(None, ("groups", "wide")),
            P(("groups", "wide"), "tp"),
            P(),
            P(None, None, "tp"),
            P("tp", None),
            P(),
            P(None, "tp"),
            P("tp", None),
            P(),
            P("wide", "tp"),
            P("wide", "tp"),
            P("wide", "tp"),
        ),
        out_specs=(
            P(("groups", "wide"), "tp"),
            P(("groups", "wide"), "tp"),
            P(("groups", "wide"), "tp"),
        ),
        check_vma=False,
    )
```

profile of v0, /device:TPU:0, one launch (start us, length us, event | category | flops | bytes accessed | tf_op | source)
XLA Modules:
  0.0 468.5 jit_solution(7635394783025104218)
XLA Ops:
  7.2 1.4 convert_reduce_fusion
  8.6 1.4 fusion.7
  10.1 2.0 convolution_convert_fusion.2
  12.1 0.2 copy.34
  12.3 0.8 reshape.470
  13.1 0.4 fusion.114
  13.7 0.4 fusion.116
  14.0 0.3 fusion.12
  14.3 0.3 fusion.15
  14.7 0.1 copy.39
  14.8 0.2 reshape.471
  15.0 0.2 copy-done.4
  15.2 1.3 convolution_convert_fusion.1
  17.1 42.7 %all-reduce.2.cloned.1.call-done = bf16[256,1280]{1,0:T(8,128)(2,1)} async-done(((bf16[256,1280]{1,0:T(8,128)(2,1)}), bf16[256,1280]{1,0:T(8,128)(2,1)}) %all-reduce.2.cloned.1.call-update) | async-done | bytes 655376 | tf_op jit(solution)/shard_map/psum | solution.py:146
  59.8 1.4 fusion.14
  61.2 1.4 multiply_reduce_fusion
  62.7 0.3 multiply_convert_fusion
  63.0 0.4 reshape.472
  63.4 10.2 %convolution_convert_fusion = bf16[64,8192]{1,0:T(8,128)(2,1)} fusion(bf16[640,8192]{1,0:T(8,128)(2,1)} %param.25, bf16[64,5120]{1,0:T(8,128)(2,1)S(1)} %reshape.472, bf16[5120,640]{1,0:T(8,128)(2,1)} %param.24), kind=kOutput, calls=%fused_computation.8 | convolution fusion | flops 1093705728 | bytes 18743296 | tf_op jit(solution)/shard_map/dot_general | solution.py:154
  74.3 26.4 %reduce-scatter.2.cloned.1.call-done = bf16[64,2048]{1,0:T(8,128)(2,1)} async-done(((bf16[64,8192]{1,0:T(8,128)(2,1)}), bf16[64,2048]{1,0:T(8,128)(2,1)}) %reduce-scatter.2.cloned.1.call-update) | async-done | bytes 262160 | tf_op jit(solution)/shard_map/reduce_scatter | solution.py:158
  100.6 2.0 gather_fusion
  102.6 0.8 select_select_fusion.1
  103.4 3.4 all-to-all-start
  106.9 5.9 %all-to-all-done = bf16[4,16,2048]{2,1,0:T(8,128)(2,1)S(1)} async-done(((bf16[4,16,2048]{2,1,0:T(8,128)(2,1)}), bf16[4,16,2048]{2,1,0:T(8,128)(2,1)S(1)}, u32[]{:S(2)}, u32[]{:S(2)}) %all-to-all-start) | async-done | bytes 262176 | tf_op jit(solution)/shard_map/all_to_all | solution.py:162
  112.8 2.5 gather_fusion.1
  115.3 3.3 select_select_fusion
  118.6 0.5 all-gather.9.cloned.1.call-update
  119.2 0.5 all-gather.11.cloned.1.call-update
  119.8 0.2 all-gather.7.cloned.1.call-start
  120.0 0.3 all-gather.7.cloned.1.call-update
  120.4 0.3 convert_multiply_fusion.2
  120.7 1.1 fusion.23
  121.9 0.1 copy.41
  122.1 143.8 %all-gather.5.cloned.1.call-done = bf16[512,8192]{1,0:T(8,128)(2,1)} async-done(((bf16[512,2048]{1,0:T(8,128)(2,1)}), bf16[512,8192]{1,0:T(8,128)(2,1)}) %all-gather.5.cloned.1.call-update) | async-done | bytes 8388624 | tf_op jit(solution)/shard_map/all_gather | solution.py:164
  265.9 5.1 %fusion.1 = f32[512]{0:T(512)S(1)} fusion(bf16[512,8192]{1,0:T(8,128)(2,1)} %all-gather.5.cloned.1.call-done), kind=kLoop, calls=%fused_computation.5 | loop fusion | flops 12582400 | bytes 8390656 | tf_op jit(solution)/shard_map/reduce_sum | solution.py:25
  271.0 29.0 %all-gather.9.cloned.1.call-done = bf16[8192,256]{1,0:T(8,128)(2,1)} async-done(((bf16[2048,256]{1,0:T(8,128)(2,1)}), bf16[8192,256]{1,0:T(8,128)(2,1)}) %all-gather.9.cloned.1.call-update) | async-done | bytes 4194320 | tf_op jit(solution)/shard_map/all_gather | solution.py:168
  300.0 7.6 %fusion.109 = f32[512,256]{0,1:T(8,128)S(1)} fusion(bf16[8192,256]{1,0:T(8,128)(2,1)} %all-gather.9.cloned.1.call-done, bf16[512,8192]{1,0:T(8,128)(2,1)} %all-gather.5.cloned.1.call-done, f32[8192]{0:T(1024)S(1)} %copy-done.9, f32[512]{0:T(512)S(1)} %add_rsqrt_fusion), kind=kOutput, calls=%fused_computation.191 | convolution fusion | flops 2164260864 | bytes 13142016 | tf_op jit(solution)/shard_map/dot_general | solution.py:173
  307.7 0.1 fusion.20
  307.8 0.8 copy.42
  308.7 27.2 %all-gather.11.cloned.1.call-done = bf16[8192,256]{1,0:T(8,128)(2,1)} async-done(((bf16[2048,256]{1,0:T(8,128)(2,1)}), bf16[8192,256]{1,0:T(8,128)(2,1)}) %all-gather.11.cloned.1.call-update) | async-done | bytes 4194320 | tf_op jit(solution)/shard_map/all_gather | solution.py:169
  335.9 7.7 %convolution_convert_fusion.4 = bf16[512,256]{1,0:T(8,128)(2,1)} fusion(bf16[8192,256]{1,0:T(8,128)(2,1)} %all-gather.11.cloned.1.call-done, bf16[512,8192]{1,0:T(8,128)(2,1)} %all-gather.5.cloned.1.call-done, f32[8192]{0:T(1024)S(1)} %copy-done.9, f32[512]{0:T(512)S(1)} %add_rsqrt_fusion), kind=kOutput, calls=%fused_computation.34 | convolution fusion | flops 2164391936 | bytes 12879872 | tf_op jit(solution)/shard_map/dot_general | solution.py:173
  343.6 99.7 %all-gather.7.cloned.1.call-done = bf16[8192,1024]{1,0:T(8,128)(2,1)} async-done(((bf16[2048,1024]{1,0:T(8,128)(2,1)}), bf16[8192,1024]{1,0:T(8,128)(2,1)}) %all-gather.7.cloned.1.call-update) | async-done | bytes 16777232 | tf_op jit(solution)/shard_map/all_gather | solution.py:167
  443.2 14.7 %fusion.111 = f32[512,1024]{1,0:T(8,128)S(1)} fusion(bf16[8192,1024]{1,0:T(8,128)(2,1)} %all-gather.7.cloned.1.call-done, bf16[512,8192]{1,0:T(8,128)(2,1)} %all-gather.5.cloned.1.call-done, f32[8192]{0:T(1024)S(1)} %copy-done.9, f32[512]{0:T(512)S(1)} %add_rsqrt_fusion), kind=kOutput, calls=%fused_computation.192 | convolution fusion | flops 8606711808 | bytes 27297792 | tf_op jit(solution)/shard_map/dot_general | solution.py:173
  458.0 0.5 copy.48
  458.5 0.7 slice_negate_fusion
  459.2 0.6 maximum_multiply_fusion
  459.8 0.1 mul.194
  459.9 1.7 fusion.4
  (66 shorter events, 1.9 us)
Async XLA Ops:
  7.2 2.9 copy-start
  7.2 52.6 %all-reduce.2.cloned.1.call-start = ((), (), s32[]{:S(2)}) async-start(), calls=%async_computation.2 | async-start | bytes 1310720 | tf_op jit(solution)/shard_map/psum | solution.py:146
  12.1 1.4 copy-start.8
  14.0 1.1 copy-start.4
  14.6 2.0 copy-start.7
  14.7 45.2 %copy-start.2 = (bf16[256,1280]{1,0:T(8,128)(2,1)S(1)}, bf16[256,1280]{1,0:T(8,128)(2,1)}, u32[]{:S(2)}) copy-start(bf16[256,1280]{1,0:T(8,128)(2,1)} %param.15) | copy-start | bytes 1966084
  15.2 47.5 %copy-start.5 = (f32[1280]{0:T(1024)S(1)}, f32[1280]{0:T(1024)}, u32[]{:S(2)}) copy-start(f32[1280]{0:T(1024)} %param.23) | copy-start | bytes 15364
  16.5 84.1 %reduce-scatter.2.cloned.1.call-start = ((), (), s32[]{:S(2)}) async-start(), calls=%async_computation.3 | async-start | bytes 1310720 | tf_op jit(solution)/shard_map/reduce_scatter | solution.py:158
  59.8 2.9 copy-start.3
  103.4 9.4 %all-to-all-start = ((bf16[4,16,2048]{2,1,0:T(8,128)(2,1)}), bf16[4,16,2048]{2,1,0:T(8,128)(2,1)S(1)}, u32[]{:S(2)}, u32[]{:S(2)}) async-start(bf16[4,16,2048]{2,1,0:T(8,128)(2,1)} %select_select_fusion.1), calls=%async_computation.1 | async-start | bytes 524288 | tf_op jit(solution)/shard_map/all_to_all | solution.py:162
  106.8 159.1 %all-gather.5.cloned.1.call-start = ((), (), s32[]{:S(2)}) async-start(), calls=%async_computation.4 | async-start | bytes 10485760 | tf_op jit(solution)/shard_map/all_gather | solution.py:164
  118.6 181.4 %all-gather.9.cloned.1.call-start = ((), (), s32[]{:S(2)}) async-start(), calls=%async_computation.6 | async-start | bytes 5242880 | tf_op jit(solution)/shard_map/all_gather | solution.py:168
  119.2 216.8 %all-gather.11.cloned.1.call-start = ((), (), s32[]{:S(2)}) async-start(), calls=%async_computation.7 | async-start | bytes 5242880 | tf_op jit(solution)/shard_map/all_gather | solution.py:169
  119.7 0.7 copy-start.6
  119.8 323.5 %all-gather.7.cloned.1.call-start = ((), (), s32[]{:S(2)}) async-start(), calls=%async_computation.5 | async-start | bytes 20971520 | tf_op jit(solution)/shard_map/all_gather | solution.py:167
  122.1 177.9 %copy-start.9 = (f32[8192]{0:T(1024)S(1)}, f32[8192]{0:T(1024)}, u32[]{:S(2)}) copy-start(f32[8192]{0:T(1024)} %param.26) | copy-start | bytes 98308
  459.9 1.7 copy-start.1
Sparse Core Ops, SparseCore 0:
  16.7 43.0 all-reduce.1
  73.8 26.8 reduce-scatter.1
  118.7 147.1 all-gather.4
  267.3 32.6 all-gather.8
  301.4 34.4 all-gather.10
  337.3 105.8 all-gather.6
where the time goes:
time: 469 us; the launch traced here: 468 us
  waiting for transfers between devices  376 us (80%)
  matrix products  44.5 us (9%)
  other arithmetic  20.6 us (4%)
  between operations  14.5 us (3%)
  local copies, waits for them, and re-layouts  9 us (2%)
    all_gather x1, waiting for transfers between devices, per_device(): prompt_rows = lax.all_gather(prompt_slice, 'tp', axis=1, tiled=True)  144 us
    all_gather x1, waiting for transfers between devices, per_device(): lax.all_gather(llm_query, 'wide', axis=0, tiled=True)  99.7 us
    psum x1, waiting for transfers between devices, per_device(): lax.psum(partial_heads.astype(jnp.bfloat16), 'tp').astype(jnp.float32)  42.7 us
    dot_general x3, matrix products, per_device(): jnp.dot(normed_prompt, matrix_rows, preferred_element_type=jnp.float32)  30 us
    all_gather x1, waiting for transfers between devices, per_device(): lax.all_gather(llm_key, 'wide', axis=0, tiled=True)  29 us
    all_gather x1, waiting for transfers between devices, per_device(): lax.all_gather(llm_value, 'wide', axis=0, tiled=True)  27.2 us
    reduce_scatter x1, waiting for transfers between devices, per_device(): lax.psum_scatter(partial_visual.astype(jnp.bfloat16), 'tp', scatter_dimen...  26.4 us
    dot_general x1, matrix products, per_device(): jnp.dot(hidden, merger_down, preferred_element_type=jnp.float32)  10.2 us
  transfers between devices with their start and end apart: 7, of which 7 were waited for; matrix products, arithmetic and copies ran while one was open for 5% of the time, Pallas kernels for 0%

commit v1 on v0

--- a/solution.py
+++ b/solution.py
@@ -161,7 +161,12 @@
     outgoing = pack_rows(visual, send_index, send_live)
     incoming = lax.all_to_all(outgoing, "wide", split_axis=0, concat_axis=0, tiled=True)
     prompt_slice = place_rows(incoming, take_index, take_live, text_embeds)
-    prompt_rows = lax.all_gather(prompt_slice, "tp", axis=1, tiled=True)
+    ring = [prompt_slice]
+    for hop in range(3):
+        ring.append(lax.ppermute(ring[-1], "tp", [(dev, (dev + 1) % 4) for dev in range(4)]))
+    prompt_rows = jnp.roll(
+        jnp.concatenate(ring[::-1], axis=1), (lax.axis_index("tp") + 1) * ring[0].shape[1], axis=1
+    )
     normed_prompt = rms_norm(prompt_rows.astype(jnp.float32), llm_gain).astype(jnp.bfloat16)
     weight_rows = (
         lax.all_gather(llm_query, "wide", axis=0, tiled=True),

time: 469 us -> 324 us (0.69)
  waiting for transfers between devices: 376 us -> 217 us
  local copies, waits for them, and re-layouts: 9 us -> 25.7 us
    all_gather x1 -> x0, waiting for transfers between devices: 144 us -> none  [per_device(): prompt_rows = lax.all_gather(prompt_slice, 'tp', axis=1, tiled=True)]
    ppermute x0 -> x3, waiting for transfers between devices: none -> 142 us  [per_device(): lax.ppermute(ring[-1], 'tp', [(dev, (dev + 1) % 4) for dev in range(4)])]
    all_gather x1, waiting for transfers between devices: 99.7 us -> 0.01 us  [per_device(): lax.all_gather(llm_query, 'wide', axis=0, tiled=True)]
    all_gather x1, waiting for transfers between devices: 29 us -> 0.02 us  [per_device(): lax.all_gather(llm_key, 'wide', axis=0, tiled=True)]
    all_gather x1, waiting for transfers between devices: 27.2 us -> 0.01 us  [per_device(): lax.all_gather(llm_value, 'wide', axis=0, tiled=True)]
    unnamed x22 -> x35, local copies, waits for them, and re-layouts: 1.65 us -> 16.5 us
  transfers between devices with their start and end apart: 7 -> 9, of which waited for: 7 -> 6; matrix products, arithmetic and copies ran while one was open for 5% -> 12% of each run, Pallas kernels for 0% -> 0%
where the time goes in v1:
time: 324 us
  waiting for transfers between devices  217 us (67%)
  matrix products  44.5 us (14%)
  local copies, waits for them, and re-layouts  25.7 us (8%)
  other arithmetic  16.6 us (5%)
  between operations  16.2 us (5%)
  starting transfers between devices  3.67 us (1%)
    ppermute x3, waiting for transfers between devices, per_device(): lax.ppermute(ring[-1], 'tp', [(dev, (dev + 1) % 4) for dev in range(4)])  142 us
    psum x1, waiting for transfers between devices, per_device(): lax.psum(partial_heads.astype(jnp.bfloat16), 'tp').astype(jnp.float32)  43.2 us
    dot_general x3, matrix products, per_device(): jnp.dot(normed_prompt, matrix_rows, preferred_element_type=jnp.float32)  30 us
    reduce_scatter x1, waiting for transfers between devices, per_device(): lax.psum_scatter(partial_visual.astype(jnp.bfloat16), 'tp', scatter_dimen...  24 us
    unnamed x35, local copies, waits for them, and re-layouts  16.5 us
    dot_general x1, matrix products, per_device(): jnp.dot(hidden, merger_down, preferred_element_type=jnp.float32)  10.2 us
  transfers between devices with their start and end apart: 9, of which 6 were waited for; matrix products, arithmetic and copies ran while one was open for 12% of the time, Pallas kernels for 0%

profile of v1, /device:TPU:0, one launch (start us, length us, event | category | flops | bytes accessed | tf_op | source)
XLA Modules:
  0.0 323.5 jit_solution(11547811606439366905)
XLA Ops:
  8.1 0.9 dynamic_slice.23
  9.0 1.3 convert_reduce_fusion
  10.3 1.4 fusion.7
  11.7 2.0 convolution_convert_fusion.2
  14.0 0.8 reshape.470
  14.7 0.4 fusion.114
  15.1 0.3 fusion.12
  15.4 0.4 fusion.116
  15.8 0.3 fusion.15
  16.5 1.3 convolution_convert_fusion.1
  18.0 43.2 %all-reduce.2.cloned.1.call-done = bf16[256,1280]{1,0:T(8,128)(2,1)} async-done(((bf16[256,1280]{1,0:T(8,128)(2,1)}), bf16[256,1280]{1,0:T(8,128)(2,1)}) %all-reduce.2.cloned.1.call-update) | async-done | bytes 655376 | tf_op jit(solution)/shard_map/psum | solution.py:146
  61.2 1.4 fusion.14
  62.6 1.4 multiply_reduce_fusion
  64.1 0.3 multiply_convert_fusion
  64.4 0.4 reshape.472
  64.8 10.2 %convolution_convert_fusion = bf16[64,8192]{1,0:T(8,128)(2,1)} fusion(bf16[640,8192]{1,0:T(8,128)(2,1)} %param.25, bf16[64,5120]{1,0:T(8,128)(2,1)S(1)} %reshape.472, bf16[5120,640]{1,0:T(8,128)(2,1)} %param.24), kind=kOutput, calls=%fused_computation.8 | convolution fusion | flops 1093705728 | bytes 18743296 | tf_op jit(solution)/shard_map/dot_general | solution.py:154
  75.1 0.5 all-gather.6.cloned.1.call-update
  75.7 0.5 all-gather.8.cloned.1.call-update
  76.3 0.5 all-gather.4.cloned.1.call-update
  77.9 24.0 %reduce-scatter.2.cloned.1.call-done = bf16[64,2048]{1,0:T(8,128)(2,1)} async-done(((bf16[64,8192]{1,0:T(8,128)(2,1)}), bf16[64,2048]{1,0:T(8,128)(2,1)}) %reduce-scatter.2.cloned.1.call-update) | async-done | bytes 262160 | tf_op jit(solution)/shard_map/reduce_scatter | solution.py:158
  102.0 2.0 gather_fusion
  104.0 0.8 select_select_fusion.1
  104.8 3.4 %all-to-all-start = ((bf16[4,16,2048]{2,1,0:T(8,128)(2,1)}), bf16[4,16,2048]{2,1,0:T(8,128)(2,1)S(1)}, u32[]{:S(2)}, u32[]{:S(2)}) async-start(bf16[4,16,2048]{2,1,0:T(8,128)(2,1)} %select_select_fusion.1), calls=%async_computation.1 | async-start | bytes 524288 | tf_op jit(solution)/shard_map/all_to_all | solution.py:162
  108.2 6.0 %all-to-all-done = bf16[4,16,2048]{2,1,0:T(8,128)(2,1)S(1)} async-done(((bf16[4,16,2048]{2,1,0:T(8,128)(2,1)}), bf16[4,16,2048]{2,1,0:T(8,128)(2,1)S(1)}, u32[]{:S(2)}, u32[]{:S(2)}) %all-to-all-start) | async-done | bytes 262176 | tf_op jit(solution)/shard_map/all_to_all | solution.py:162
  114.2 3.3 %gather_fusion.1 = bf16[512,2048]{1,0:T(8,128)(2,1)} fusion(bf16[64,2048]{1,0:T(8,128)(2,1)S(1)} %bitcast.76, s32[1024]{0:T(1024)S(1)} %pad_clamp_fusion), kind=kCustom, calls=%fused_computation.1 | custom fusion | bytes 4196352 | tf_op jit(solution)/shard_map/jit(_take)/gather | solution.py:101
  117.5 2.8 select_select_fusion
  120.4 48.7 %collective-permute-done = bf16[512,2048]{1,0:T(8,128)(2,1)S(1)} collective-permute-done((bf16[512,2048]{1,0:T(8,128)(2,1)S(1)}, bf16[512,2048]{1,0:T(8,128)(2,1)S(1)}, u32[]{:S(2)}, u32[]{:S(2)}) %collective-permute-start) | collective-permute-done | bytes 2097184 | tf_op jit(solution)/shard_map/ppermute | solution.py:166
  169.0 1.3 copy-done.3
  170.3 47.9 %collective-permute-done.1 = bf16[512,2048]{1,0:T(8,128)(2,1)} collective-permute-done((bf16[512,2048]{1,0:T(8,128)(2,1)S(1)}, bf16[512,2048]{1,0:T(8,128)(2,1)}, u32[]{:S(2)}, u32[]{:S(2)}) %collective-permute-start.1) | collective-permute-done | bytes 2097184 | tf_op jit(solution)/shard_map/ppermute | solution.py:166
  218.3 0.3 convert_multiply_fusion.2
  218.6 1.1 fusion.23
  220.0 45.5 %collective-permute-done.2 = bf16[512,2048]{1,0:T(8,128)(2,1)} collective-permute-done((bf16[512,2048]{1,0:T(8,128)(2,1)}, bf16[512,2048]{1,0:T(8,128)(2,1)}, u32[]{:S(2)}, u32[]{:S(2)}) %collective-permute-start.2) | collective-permute-done | bytes 2097184 | tf_op jit(solution)/shard_map/ppermute | solution.py:166
  265.5 1.7 constant_dynamic-update-slice_fusion.7
  267.2 1.9 constant_dynamic-update-slice_fusion.6
  269.1 0.3 copy-done.4
  269.8 1.7 constant_dynamic-update-slice_fusion.3
  271.6 1.7 constant_dynamic-update-slice_fusion.2
  273.3 0.2 constant_dynamic-update-slice_fusion.1
  273.7 5.7 %copy-done.5 = bf16[512,16384]{1,0:T(8,128)(2,1)} copy-done((bf16[512,16384]{1,0:T(8,128)(2,1)}, bf16[512,16384]{1,0:T(8,128)(2,1)S(1)}, u32[]{:S(2)}) %copy-start.5) | copy-done | bytes 16777240
  279.4 1.7 fusion.1
  281.2 7.6 %fusion.109 = f32[512,256]{0,1:T(8,128)S(1)} fusion(bf16[8192,256]{1,0:T(8,128)(2,1)} %all-gather.6.cloned.1.call-done, f32[8192]{0:T(1024)S(1)} %copy-done.12, f32[512]{0:T(512)S(1)} %add_rsqrt_fusion, bf16[512,16384]{1,0:T(8,128)(2,1)} %copy-done.5, s32[]{:T(128)S(6)} %select_n.167), kind=kOutput, calls=%fused_computation.199 | convolution fusion | flops 2164260864 | bytes 13142020 | tf_op jit(solution)/shard_map/dot_general | solution.py:178
  289.0 0.8 copy.42
  289.9 7.7 %convolution_convert_fusion.4 = bf16[512,256]{1,0:T(8,128)(2,1)} fusion(bf16[8192,256]{1,0:T(8,128)(2,1)} %all-gather.8.cloned.1.call-done, f32[8192]{0:T(1024)S(1)} %copy-done.12, f32[512]{0:T(512)S(1)} %add_rsqrt_fusion, bf16[512,16384]{1,0:T(8,128)(2,1)} %copy-done.5, s32[]{:T(128)S(6)} %select_n.167), kind=kOutput, calls=%fused_computation.34 | convolution fusion | flops 2164391936 | bytes 12879876 | tf_op jit(solution)/shard_map/dot_general | solution.py:178
  297.6 14.7 %fusion.111 = f32[512,1024]{1,0:T(8,128)S(1)} fusion(bf16[8192,1024]{1,0:T(8,128)(2,1)} %all-gather.4.cloned.1.call-done, f32[8192]{0:T(1024)S(1)} %copy-done.12, f32[512]{0:T(512)S(1)} %add_rsqrt_fusion, bf16[512,16384]{1,0:T(8,128)(2,1)} %copy-done.5, s32[]{:T(128)S(6)} %select_n.167), kind=kOutput, calls=%fused_computation.200 | convolution fusion | flops 8606711808 | bytes 27297796 | tf_op jit(solution)/shard_map/dot_general | solution.py:178
  312.3 0.5 copy.48
  312.8 0.7 slice_negate_fusion
  313.5 0.6 maximum_multiply_fusion
  314.2 1.7 fusion.4
  (83 shorter events, 3.4 us)
Async XLA Ops:
  8.0 3.7 %copy-start = (bf16[1280,3,320]{0,2,1:T(8,128)(2,1)S(1)}, bf16[1280,3,320]{0,2,1:T(8,128)(2,1)}, u32[]{:S(2)}) copy-start(bf16[1280,3,320]{0,2,1:T(8,128)(2,1)} %param.21) | copy-start | bytes 7372804
  8.0 53.2 %all-reduce.2.cloned.1.call-start = ((), (), s32[]{:S(2)}) async-start(), calls=%async_computation.2 | async-start | bytes 1310720 | tf_op jit(solution)/shard_map/psum | solution.py:146
  15.4 1.1 copy-start.7
  15.8 45.4 %copy-start.2 = (bf16[256,1280]{1,0:T(8,128)(2,1)S(1)}, bf16[256,1280]{1,0:T(8,128)(2,1)}, u32[]{:S(2)}) copy-start(bf16[256,1280]{1,0:T(8,128)(2,1)} %param.15) | copy-start | bytes 1966084
  16.5 47.5 %copy-start.8 = (f32[1280]{0:T(1024)S(1)}, f32[1280]{0:T(1024)}, u32[]{:S(2)}) copy-start(f32[1280]{0:T(1024)} %param.23) | copy-start | bytes 15364
  17.9 84.1 %reduce-scatter.2.cloned.1.call-start = ((), (), s32[]{:S(2)}) async-start(), calls=%async_computation.3 | async-start | bytes 1310720 | tf_op jit(solution)/shard_map/reduce_scatter | solution.py:158
  61.2 2.9 copy-start.6
  75.0 206.1 %all-gather.6.cloned.1.call-start = ((), (), s32[]{:S(2)}) async-start(), calls=%async_computation.5 | async-start | bytes 5242880 | tf_op jit(solution)/shard_map/all_gather | solution.py:173
  75.6 1.2 copy-start.10
  75.6 1.2 copy-start.11
  75.6 214.3 %all-gather.8.cloned.1.call-start = ((), (), s32[]{:S(2)}) async-start(), calls=%async_computation.6 | async-start | bytes 5242880 | tf_op jit(solution)/shard_map/all_gather | solution.py:174
  76.2 221.3 %all-gather.4.cloned.1.call-start = ((), (), s32[]{:S(2)}) async-start(), calls=%async_computation.4 | async-start | bytes 20971520 | tf_op jit(solution)/shard_map/all_gather | solution.py:172
  104.8 9.4 %all-to-all-start = ((bf16[4,16,2048]{2,1,0:T(8,128)(2,1)}), bf16[4,16,2048]{2,1,0:T(8,128)(2,1)S(1)}, u32[]{:S(2)}, u32[]{:S(2)}) async-start(bf16[4,16,2048]{2,1,0:T(8,128)(2,1)} %select_select_fusion.1), calls=%async_computation.1 | async-start | bytes 524288 | tf_op jit(solution)/shard_map/all_to_all | solution.py:162
  117.5 100.8 %copy-start.9 = (s32[3,512]{1,0:T(4,128)S(1)}, s32[3,512]{1,0:T(4,128)}, u32[]{:S(2)}) copy-start(s32[3,512]{1,0:T(4,128)} %param.18) | copy-start | bytes 18436
  120.3 48.7 %collective-permute-start = (bf16[512,2048]{1,0:T(8,128)(2,1)S(1)}, bf16[512,2048]{1,0:T(8,128)(2,1)S(1)}, u32[]{:S(2)}, u32[]{:S(2)}) collective-permute-start(bf16[512,2048]{1,0:T(8,128)(2,1)S(1)} %select_select_fusion), channel_id=1, source_target_pairs={{0,1},{1,2},{2,3},{3,0},{4,5},{5,6},{6,7},{7,4},{8,9},{9,10},{10,1... | collective-permute-start | bytes 6291464 | tf_op jit(solution)/shard_map/ppermute | solution.py:166
  169.0 1.3 copy-start.3
  170.3 47.9 %collective-permute-start.1 = (bf16[512,2048]{1,0:T(8,128)(2,1)S(1)}, bf16[512,2048]{1,0:T(8,128)(2,1)}, u32[]{:S(2)}, u32[]{:S(2)}) collective-permute-start(bf16[512,2048]{1,0:T(8,128)(2,1)S(1)} %collective-permute-done), channel_id=1, source_target_pairs={{0,1},{1,2},{2,3},{3,0},{4,5},{5,6},{6,7},{7,4},{8,9},{9,10},{10,1... | collective-permute-start | bytes 6291464 | tf_op jit(solution)/shard_map/ppermute | solution.py:166
  218.2 47.3 %collective-permute-start.2 = (bf16[512,2048]{1,0:T(8,128)(2,1)}, bf16[512,2048]{1,0:T(8,128)(2,1)}, u32[]{:S(2)}, u32[]{:S(2)}) collective-permute-start(bf16[512,2048]{1,0:T(8,128)(2,1)} %collective-permute-done.1), channel_id=1, source_target_pairs={{0,1},{1,2},{2,3},{3,0},{4,5},{5,6},{6,7},{7,4},{8,9},{9,10},{10,1... | collective-permute-start | bytes 6291464 | tf_op jit(solution)/shard_map/ppermute | solution.py:166
  267.2 2.2 copy-start.4
  273.7 5.7 %copy-start.5 = (bf16[512,16384]{1,0:T(8,128)(2,1)}, bf16[512,16384]{1,0:T(8,128)(2,1)S(1)}, u32[]{:S(2)}) copy-start(bf16[512,16384]{1,0:T(8,128)(2,1)S(1)} %constant_dynamic-update-slice_fusion) | copy-start | bytes 50331652
  279.4 1.8 copy-start.12
  314.2 1.7 copy-start.1
Sparse Core Ops, SparseCore 0:
  18.0 43.0 all-reduce.1
  75.1 26.7 reduce-scatter.1
Sparse Core Ops, SparseCore 1:
  77.1 33.8 all-gather.5
  112.4 35.1 all-gather.7
  149.0 105.7 all-gather.3
